TPU v7x, 32 devices: a whole 2x2x4 slice. The times are simulated.
32 devices in a mesh: replica: 4 (over y, core), table: 8 (over z, x).
Axes of the slice: x: 2, y: 2, z: 4, core: 2. Of those that a mesh axis runs over, the one named last changes fastest.
Arguments:
- cache: float32 [768, 16384], P('table', 'replica'), may hold values from -6 to 6
- accum: float32 [768, 16384], P('table', 'replica'), may hold values from 0.5 to 8
- row_ids: int32 [4, 8, 128], P('replica'), may hold values from 0 to 4095
- lengths: int32 [4, 8], P('replica'), may hold values from 1 to 128, 614 in all within a row
- seq_slot: int32 [4, 8], P('replica'), may hold values from 0 to 7, each once within a row
- block_mask: int32 [4, 8, 2, 2], P('replica'), may hold values 0 or 1
- cotangent: bfloat16 [4, 1024, 768], P('replica', 'table'), may hold values from -6 to 6
- w_uqkv: bfloat16 [768, 3072], P('replica'), may hold values from -0.21875 to 0.21875
- w_out: bfloat16 [768, 768], P('replica'), may hold values from -0.21875 to 0.21875
- w2_accum: float32 [768, 768], P('replica', 'table'), may hold values from 81.92 to 8192
Outputs:
- cache_new: float32 [768, 16384], P('table', 'replica')
- accum_new: float32 [768, 16384], P('table', 'replica')
- w2_step: float32 [768, 768], P('replica', 'table')
Inputs may be any that keep to these rules, and one draw needn't show every extreme that they name: `lengths`: in every replica group some sequence has length 128. `seq_slot`: each row names every slot once.
All inputs are finite; a program needn't handle non-finite values. No bound on the sum of `block_mask` on one device may be relied on, other than what follows from the above.
Results may differ from a plain program's by a relative error of at most 0.012.
Values may be sent and summed in bfloat16 or wider, within the bound.
A program may use at most 64 MiB of HBM per device.

v0:
```python
from functools import partial
import jax
import jax.numpy as jnp
from jax import lax
from jax.sharding import PartitionSpec as P

D = 768
HEADS = 12
HEAD_DIM = 64
SEQ_DEV = 1
SEQ_LEN = 128
CAP = 128
EPS_NORM = 1e-05
EPS_ATTN = 1e-06
STEP_SIZE = 0.5


def normalize(row_data):
    centred = row_data - jnp.mean(row_data, axis=-1, keepdims=True)
    variance = jnp.mean(centred * centred, axis=-1, keepdims=True)
    return centred / jnp.sqrt(variance + EPS_NORM)


def pattern_mask(lengths_at, blocks_at, seq_len):
    block_count = blocks_at.shape[-1]
    block_width = seq_len // block_count
    places = jnp.arange(seq_len, dtype=jnp.int32)
    block_of = places // block_width
    same_block = block_of[:, None] == block_of[None, :]
    chosen = jnp.repeat(jnp.repeat(blocks_at, block_width, axis=1), block_width, axis=2) > 0
    chosen = chosen | same_block[None]
    causal = places[None, :] <= places[:, None]
    inside = places[None, :] < lengths_at[:, None]
    allowed = chosen & causal[None] & inside[:, :, None] & inside[:, None, :]
    return (allowed.astype(jnp.float32), inside)


def attention_branch(hidden_pre, allowed):
    slot_count = allowed.shape[0]
    seq_len = allowed.shape[1]
    projected = jax.nn.silu(hidden_pre).astype(jnp.bfloat16)
    gate_u = projected[:, :D]
    queries = projected[:, D : 2 * D].reshape(slot_count, seq_len, HEADS, HEAD_DIM)
    key_rows = projected[:, 2 * D : 3 * D].reshape(slot_count, seq_len, HEADS, HEAD_DIM)
    value_rows = projected[:, 3 * D :].reshape(slot_count, seq_len, HEADS, HEAD_DIM)
    scores = jnp.einsum(
        "sihd,sjhd->shij", queries, key_rows, preferred_element_type=jnp.float32
    ) * HEAD_DIM ** (-0.5)
    weights = (jax.nn.silu(scores) * allowed[:, None]).astype(jnp.bfloat16)
    attended = jnp.einsum(
        "shij,sjhd->sihd", weights, value_rows, preferred_element_type=jnp.float32
    )
    attended = attended.reshape(slot_count * seq_len, D)
    centred_att = attended - jnp.mean(attended, axis=-1, keepdims=True)
    inverse_dev = 1.0 / jnp.sqrt(
        jnp.mean(centred_att * centred_att, axis=-1, keepdims=True) + EPS_ATTN
    )
    return centred_att * inverse_dev * gate_u.astype(jnp.float32)


def body(cache, accum, row_ids, lengths, seq_slot, block_mask, cotangent, w_uqkv, w_out, w2_accum):
    tables = lax.axis_size("table")
    table_index = lax.axis_index("table")
    columns = cache.shape[0]
    seq_count = seq_slot.shape[1]
    sequence_ids = jnp.arange(seq_count, dtype=jnp.int32)
    matches = (seq_slot[0][:, None] == sequence_ids[None, :]).astype(jnp.int32)
    seq_at = jnp.sum(sequence_ids[:, None] * matches, axis=0)
    lengths_at = jnp.sum(lengths[0][:, None] * matches, axis=0)
    slot_ids = row_ids[0][seq_at].reshape(-1)
    own_first = table_index * SEQ_DEV
    own_lengths = lax.dynamic_slice_in_dim(lengths_at, own_first, SEQ_DEV, 0)
    own_blocks = lax.dynamic_slice_in_dim(block_mask[0][seq_at], own_first, SEQ_DEV, 0)
    allowed, inside = pattern_mask(own_lengths, own_blocks, SEQ_LEN)
    picked = jnp.take(cache, slot_ids, axis=1).astype(jnp.bfloat16).reshape(columns, tables, CAP)
    arrived = lax.all_to_all(picked, "table", split_axis=1, concat_axis=0, tiled=True)
    embedded = arrived.reshape(D, CAP).T
    row_float = embedded.astype(jnp.float32)
    normed = normalize(row_float).astype(jnp.bfloat16)
    full_uqkv = lax.all_gather(w_uqkv, "replica", axis=0, tiled=True)
    hidden_pre = jnp.dot(normed, full_uqkv, preferred_element_type=jnp.float32)
    live_cot = cotangent[0] * inside.reshape(-1)[:, None].astype(jnp.bfloat16)
    d_gated = lax.dot_general(
        live_cot,
        lax.all_gather(w_out, "replica", axis=0, tiled=True),
        (((1,), (1,)), ((), ())),
        preferred_element_type=jnp.float32,
    )
    gated_raw, branch_vjp = jax.vjp(partial(attention_branch, allowed=allowed), hidden_pre)
    gated = gated_raw.astype(jnp.bfloat16)
    d_hidden = branch_vjp(d_gated)[0].astype(jnp.bfloat16)
    d_normed = lax.dot_general(
        d_hidden, full_uqkv, (((1,), (1,)), ((), ())), preferred_element_type=jnp.float32
    )
    _, norm_vjp = jax.vjp(normalize, row_float)
    row_grad = live_cot.astype(jnp.float32) + norm_vjp(d_normed)[0]
    sending = row_grad.T.reshape(tables, columns, CAP)
    returned = lax.all_to_all(sending, "table", split_axis=0, concat_axis=2, tiled=True).reshape(
        columns, tables * CAP
    )
    grad_cols = jnp.zeros_like(cache).at[:, slot_ids].add(returned)
    accum_next = accum + grad_cols * grad_cols
    cache_next = cache - STEP_SIZE * grad_cols / jnp.sqrt(accum_next)
    full_grad = lax.dot_general(
        gated, live_cot, (((0,), (0,)), ((), ())), preferred_element_type=jnp.float32
    )
    by_columns = lax.psum_scatter(full_grad, "table", scatter_dimension=1, tiled=True)
    summed = lax.psum_scatter(by_columns, "replica", scatter_dimension=0, tiled=True)
    w2_step = summed / jnp.sqrt(w2_accum + summed * summed)
    return (cache_next, accum_next, w2_step)


def solution(mesh):
    return jax.shard_map(
        body,
        mesh=mesh,
        in_specs=(
            P("table", "replica"),
            P("table", "replica"),
            P("replica", None, None),
            P("replica", None),
            P("replica", None),
            P("replica", None, None, None),
            P("replica", "table", None),
            P("replica", None),
            P("replica", None),
            P("replica", "table"),
        ),
        out_specs=(P("table", "replica"), P("table", "replica"), P("replica", "table")),
        check_vma=False,
    )
```

profile of v0, /device:TPU:0, one launch (start us, length us, event | category | flops | bytes accessed | tf_op | source)
XLA Modules:
  0.0 180.1 jit_solution(12258738646778073409)
XLA Ops:
  7.9 1.8 %copy.119 = f32[96,4096]{0,1:T(8,128)S(1)} copy(f32[96,4096]{1,0:T(8,128)} %param.10) | data formatting | bytes 3145728 | tf_op args[0]
  10.5 2.9 %gather_fusion.1 = bf16[1024,96]{1,0:T(8,128)(2,1)S(1)} fusion(f32[96,4096]{0,1:T(8,128)S(1)} %copy.119, s32[1024]{0:T(1024)S(1)} %broadcast_clamp_fusion), kind=kCustom, calls=%fused_computation.1 | custom fusion | bytes 397312 | tf_op jit(solution)/shard_map/jit(_take)/gather | solution.py:75
  14.3 7.3 %all-to-all-start = ((bf16[96,8,128]{2,0,1:T(8,128)(2,1)}), bf16[96,8,128]{2,0,1:T(8,128)(2,1)S(1)}, u32[]{:S(2)}, u32[]{:S(2)}) async-start(bf16[96,8,128]{2,0,1:T(8,128)(2,1)} %select_convert_fusion), calls=%async_computation | async-start | bytes 393216 | tf_op jit(solution)/shard_map/all_to_all | solution.py:76
  25.5 4.1 %all-to-all-done = bf16[96,8,128]{2,0,1:T(8,128)(2,1)S(1)} async-done(((bf16[96,8,128]{2,0,1:T(8,128)(2,1)}), bf16[96,8,128]{2,0,1:T(8,128)(2,1)S(1)}, u32[]{:S(2)}, u32[]{:S(2)}) %all-to-all-start) | async-done | bytes 196640 | tf_op jit(solution)/shard_map/all_to_all | solution.py:76
  30.6 19.1 %all-gather.5.cloned.1.call-done = bf16[768,3072]{1,0:T(8,128)(2,1)} async-done(((bf16[192,3072]{1,0:T(8,128)(2,1)}), bf16[768,3072]{1,0:T(8,128)(2,1)}) %all-gather.5.cloned.1.call-update) | async-done | bytes 4718608 | tf_op jit(solution)/shard_map/all_gather | solution.py:80
  49.7 4.4 %multiply_convert_fusion = (bf16[128,3072]{1,0:T(8,128)(2,1)S(1)}, f32[128,3072]{1,0:T(8,128)}) fusion(bf16[768,3072]{1,0:T(8,128)(2,1)} %all-gather.5.cloned.1.call-done, f32[768,128]{0,1:T(8,128)S(1)} %copy.103, f32[128]{0:T(128)S(1)} %get-tuple-element.31, f32[128]{0:T(128)S(1)} %broadcast_multiply_fusion.1), kind=kOutput, calls=%fused_computation.12 | convolution fusion | flops 606240768 | bytes 7472128 | tf_op jit(solution)/shard_map/dot_general | solution.py:81
  54.1 0.9 copy-done.2
  56.2 1.3 multiply_convert_fusion.1
  57.6 1.0 fusion.52
  60.1 8.7 %all-gather.3.cloned.1.call-done = bf16[768,768]{1,0:T(8,128)(2,1)} async-done(((bf16[192,768]{1,0:T(8,128)(2,1)}), bf16[768,768]{1,0:T(8,128)(2,1)}) %all-gather.3.cloned.1.call-update) | async-done | bytes 1179664 | tf_op jit(solution)/shard_map/all_gather | solution.py:85
  68.8 1.9 %multiply_reduce_fusion = (f32[128]{0:T(128)S(1)}, f32[128,768]{1,0:T(8,128)S(1)}) fusion(f32[128,768]{1,0:T(8,128)S(1)} %copy.110, f32[128]{0:T(128)S(1)} %broadcast_multiply_fusion, bf16[128,3072]{1,0:T(8,128)(2,1)} %copy-done.2, bf16[768,768]{1,0:T(8,128)(2,1)} %all-gather.3.cloned.1.call-done, bf16[1,128,768]{2,1,0:T(8,128)(2,1)S(1)} %copy-done.3, ...), kind=kOutput, calls=%fused_computation.56 | convolution fusion | flops 151584640 | bytes 2360576 | tf_op jit(solution)/shard_map/dot_general | solution.py:83
  71.8 3.0 %fusion.28 = f32[768,768]{0,1:T(8,128)} fusion(f32[128,768]{1,0:T(8,128)S(1)} %copy.110, f32[128]{0:T(128)S(1)} %broadcast_multiply_fusion, f32[128]{0:T(128)S(1)} %get-tuple-element.33, bf16[1,128,768]{2,1,0:T(8,128)(2,1)S(1)} %copy-done.3, bf16[128,3072]{1,0:T(8,128)(2,1)} %copy-done.2, bf16[128]{0:T(256)(128)(2,1)S(1)} %fusion.48), kind=kOutput, calls=%fused_computation.59 | convolution fusion | flops 151584768 | bytes 3147008 | tf_op jit(solution)/shard_map/dot_general | solution.py:104
  74.8 1.8 %fusion.50 = (f32[128]{0:T(128)S(1)}, f32[128,768]{1,0:T(8,128)S(1)}, bf16[128,768]{1,0:T(8,128)(2,1)}) fusion(f32[128]{0:T(128)} %get-tuple-element.32, f32[128,768]{1,0:T(8,128)S(1)} %copy.110, f32[128]{0:T(128)S(1)} %broadcast_multiply_fusion, f32[128]{0:T(128)} %copy-done.12, f32[128,768]{1,0:T(8,128)S(1)} %get-tuple-element.41, ...), kind=kLoop, calls=%fused_computation.111 | loop fusion | flops 1081216 | bytes 1574912 | tf_op jit(solution)/shard_map/transpose(jvp())/reduce_sum | solution.py:54
  77.6 1.8 fusion.11
  79.4 1.1 fusion.54
  80.5 1.8 copy.114
  82.2 1.8 %fusion.55 = bf16[12,128,64]{1,2,0:T(8,128)(2,1)} fusion(bf16[12,128,128]{2,1,0:T(8,128)(2,1)S(1)} %fusion.11, bf16[128,12,64]{0,2,1:T(8,128)(2,1)} %bitcast.125), kind=kOutput, calls=%fused_computation.116 | convolution fusion | flops 25165824 | bytes 786432 | tf_op jit(solution)/shard_map/transpose(jvp(sihd,sjhd->shij))/dot_general | solution.py:46
  84.1 1.7 copy.113
  85.8 1.2 fusion.53
  87.2 5.0 %fusion.25 = (f32[128]{0:T(128)S(1)}, f32[128,768]{1,0:T(8,128)S(1)}) fusion(f32[768,128]{0,1:T(8,128)S(1)} %copy.103, f32[128]{0:T(128)S(1)} %copy-done.23, f32[128]{0:T(128)S(1)} %copy-done.14, bf16[768,3072]{1,0:T(8,128)(2,1)} %all-gather.5.cloned.1.call-done, f32[128,3072]{1,0:T(8,128)} %get-tuple-element.35, bf16[128,768]{1,0:T(8,128)(2,1)} %get-tuple-element.26, ...), kind=kOutput, calls=%fused_computation.53 | convolution fusion | flops 611450752 | bytes 7865856 | tf_op jit(solution)/shard_map/dot_general | solution.py:92
  92.6 0.9 copy.115
  93.5 5.5 %all-to-all-start.1 = ((f32[8,96,128]{2,1,0:T(8,128)}), f32[8,96,128]{2,1,0:T(8,128)S(1)}, u32[]{:S(2)}, u32[]{:S(2)}) async-start(f32[8,96,128]{2,1,0:T(8,128)} %bitcast.40), calls=%async_computation.1 | async-start | bytes 786432 | tf_op jit(solution)/shard_map/all_to_all | solution.py:98
  99.1 2.8 %copy.118 = f32[96,4096]{0,1:T(8,128)} copy(f32[96,4096]{1,0:T(8,128)} %param.11) | data formatting | bytes 3145728 | tf_op args[1]
  102.0 13.1 %all-to-all-done.1 = f32[8,96,128]{2,1,0:T(8,128)S(1)} async-done(((f32[8,96,128]{2,1,0:T(8,128)}), f32[8,96,128]{2,1,0:T(8,128)S(1)}, u32[]{:S(2)}, u32[]{:S(2)}) %all-to-all-start.1) | async-done | bytes 393248 | tf_op jit(solution)/shard_map/all_to_all | solution.py:98
  115.6 7.4 %scatter_custom_fusion = f32[96,4096]{0,1:T(8,128)} fusion(s32[1024]{0:T(1024)S(1)} %bitcast.135, f32[1024,96]{1,0:T(8,128)S(1)} %copy.117, f32[]{:T(128)} %constant.61.clone.1), kind=kCustom, calls=%fused_computation.22 | custom fusion | flops 98304 | bytes 1572868 | tf_op jit(solution)/shard_map/scatter-add | solution.py:101
  123.0 26.4 %reduce-scatter.5.cloned.1.call-done = f32[768,96]{0,1:T(8,128)} async-done(((f32[768,768]{0,1:T(8,128)}), f32[768,96]{0,1:T(8,128)}) %reduce-scatter.5.cloned.1.call-update) | async-done | bytes 294928 | tf_op jit(solution)/shard_map/reduce_scatter | solution.py:107
  149.4 1.9 %copy.124 = f32[768,96]{1,0:T(8,128)} copy(f32[768,96]{0,1:T(8,128)} %reduce-scatter.5.cloned.1.call-done) | data formatting | bytes 589824
  151.3 4.6 %multiply_subtract_fusion = (f32[96,4096]{0,1:T(8,128)}, f32[96,4096]{0,1:T(8,128)}) fusion(f32[96,4096]{0,1:T(8,128)S(1)} %copy.119, f32[96,4096]{0,1:T(8,128)} %scatter_custom_fusion, f32[96,4096]{0,1:T(8,128)} %copy.118), kind=kLoop, calls=%fused_computation.5 | loop fusion | flops 1966080 | bytes 7864320 | tf_op jit(solution)/shard_map/sub | solution.py:103
  156.0 2.9 %copy.121 = f32[96,4096]{1,0:T(8,128)} copy(f32[96,4096]{0,1:T(8,128)} %get-tuple-element.20) | data formatting | bytes 3145728
  158.9 1.7 copy.122
  160.6 11.2 %reduce-scatter.7.cloned.1.call-done = f32[192,96]{1,0:T(8,128)} async-done(((f32[768,96]{1,0:T(8,128)}), f32[192,96]{1,0:T(8,128)}) %reduce-scatter.7.cloned.1.call-update) | async-done | bytes 73744
  171.8 1.0 copy.125
  (104 shorter events, 13.9 us)
Async XLA Ops:
  7.2 2.7 %copy-start = (s32[1,8,128]{2,1,0:T(8,128)S(1)}, s32[1,8,128]{2,1,0:T(8,128)}, u32[]{:S(2)}) copy-start(s32[1,8,128]{2,1,0:T(8,128)} %param.12) | copy-start | bytes 12292
  7.2 42.6 %all-gather.5.cloned.1.call-start = ((), (), s32[]{:S(2)}) async-start(), calls=%async_computation.5 | async-start | bytes 5898240 | tf_op jit(solution)/shard_map/all_gather | solution.py:80
  7.9 1.9 %copy-start.21 = (s32[1,8]{1,0:T(1,128)S(1)}, s32[1,8]{1,0:T(1,128)}, u32[]{:S(2)}) copy-start(s32[1,8]{1,0:T(1,128)} %param.13) | copy-start | bytes 100
  7.9 1.9 %copy-start.22 = (s32[1,8]{1,0:T(1,128)S(1)}, s32[1,8]{1,0:T(1,128)}, u32[]{:S(2)}) copy-start(s32[1,8]{1,0:T(1,128)} %param.14) | copy-start | bytes 100
  10.5 11.9 %copy-start.16 = (s32[1,8,2,2]{1,3,2,0:T(2,128)S(1)}, s32[1,8,2,2]{1,3,2,0:T(2,128)}, u32[]{:S(2)}) copy-start(s32[1,8,2,2]{1,3,2,0:T(2,128)} %param.15) | copy-start | bytes 388
  14.3 15.2 %all-to-all-start = ((bf16[96,8,128]{2,0,1:T(8,128)(2,1)}), bf16[96,8,128]{2,0,1:T(8,128)(2,1)S(1)}, u32[]{:S(2)}, u32[]{:S(2)}) async-start(bf16[96,8,128]{2,0,1:T(8,128)(2,1)} %select_convert_fusion), calls=%async_computation | async-start | bytes 393216 | tf_op jit(solution)/shard_map/all_to_all | solution.py:76
  21.6 47.2 %all-gather.3.cloned.1.call-start = ((), (), s32[]{:S(2)}) async-start(), calls=%async_computation.4 | async-start | bytes 1474560 | tf_op jit(solution)/shard_map/all_gather | solution.py:85
  22.3 127.1 %reduce-scatter.5.cloned.1.call-start = ((), (), s32[]{:S(2)}) async-start(), calls=%async_computation.6 | async-start | bytes 2654208 | tf_op jit(solution)/shard_map/reduce_scatter | solution.py:107
  29.9 24.2 %copy-start.13 = (f32[128]{0:T(128)}, f32[128]{0:T(128)S(1)}, u32[]{:S(2)}) copy-start(f32[128]{0:T(128)S(1)} %broadcast_multiply_fusion.1) | copy-start | bytes 1540
  30.1 24.0 %copy-start.19 = (f32[128]{0:T(128)}, f32[128]{0:T(128)S(1)}, u32[]{:S(2)}) copy-start(f32[128]{0:T(128)S(1)} %fusion.23) | copy-start | bytes 1540
  30.6 23.5 %copy-start.17 = (f32[128]{0:T(128)}, f32[128]{0:T(128)S(1)}, u32[]{:S(2)}) copy-start(f32[128]{0:T(128)S(1)} %get-tuple-element.31) | copy-start | bytes 1540
  54.1 0.9 copy-start.2
  56.0 1.5 copy-start.7
  56.2 1.4 copy-start.8
  56.2 1.4 copy-start.6
  57.6 1.0 copy-start.4
  57.6 11.2 %copy-start.3 = (bf16[1,128,768]{2,1,0:T(8,128)(2,1)S(1)}, bf16[1,128,768]{2,1,0:T(8,128)(2,1)}, u32[]{:S(2)}) copy-start(bf16[1,128,768]{2,1,0:T(8,128)(2,1)} %param.16) | copy-start | bytes 589828
  68.8 1.9 %copy-start.15 = (f32[128]{0:T(128)S(1)}, f32[128]{0:T(128)}, u32[]{:S(2)}) copy-start(f32[128]{0:T(128)} %fusion.22) | copy-start | bytes 1540
  71.2 0.6 copy-start.12
  76.9 0.7 copy-start.10
  77.6 1.8 %copy-start.9 = (bf16[128,768]{0,1:T(8,128)(2,1)S(1)}, bf16[128,768]{0,1:T(8,128)(2,1)}, u32[]{:S(2)}) copy-start(bf16[128,768]{0,1:T(8,128)(2,1)} %copy-done.8) | copy-start | bytes 589828
  79.4 6.4 %copy-start.5 = (bf16[12,128,128]{2,1,0:T(8,128)(2,1)S(1)}, bf16[12,128,128]{2,1,0:T(8,128)(2,1)}, u32[]{:S(2)}) copy-start(bf16[12,128,128]{2,1,0:T(8,128)(2,1)} %copy-done.4) | copy-start | bytes 1179652
  80.5 6.7 %copy-start.14 = (f32[128]{0:T(128)S(1)}, f32[128]{0:T(128)}, u32[]{:S(2)}) copy-start(f32[128]{0:T(128)} %copy-done.13) | copy-start | bytes 1540
  80.5 6.7 %copy-start.23 = (f32[128]{0:T(128)S(1)}, f32[128]{0:T(128)}, u32[]{:S(2)}) copy-start(f32[128]{0:T(128)} %get-tuple-element.30) | copy-start | bytes 1540
  87.2 5.0 %copy-start.20 = (f32[128]{0:T(128)S(1)}, f32[128]{0:T(128)}, u32[]{:S(2)}) copy-start(f32[128]{0:T(128)} %copy-done.19) | copy-start | bytes 1540
  87.2 5.0 %copy-start.18 = (f32[128]{0:T(128)S(1)}, f32[128]{0:T(128)}, u32[]{:S(2)}) copy-start(f32[128]{0:T(128)} %copy-done.17) | copy-start | bytes 1540
  93.5 21.6 %all-to-all-start.1 = ((f32[8,96,128]{2,1,0:T(8,128)}), f32[8,96,128]{2,1,0:T(8,128)S(1)}, u32[]{:S(2)}, u32[]{:S(2)}) async-start(f32[8,96,128]{2,1,0:T(8,128)} %bitcast.40), calls=%async_computation.1 | async-start | bytes 786432 | tf_op jit(solution)/shard_map/all_to_all | solution.py:98
  99.0 2.9 %copy-start.11 = (f32[192,96]{1,0:T(8,128)S(1)}, f32[192,96]{1,0:T(8,128)}, u32[]{:S(2)}) copy-start(f32[192,96]{1,0:T(8,128)} %param.19) | copy-start | bytes 221188
  99.0 72.8 %reduce-scatter.7.cloned.1.call-start = ((), (), s32[]{:S(2)}) async-start(), calls=%async_computation.7 | async-start | bytes 491520
  156.0 2.9 %copy-start.1 = (f32[96,4096]{0,1:T(8,128)S(1)}, f32[96,4096]{0,1:T(8,128)}, u32[]{:S(2)}) copy-start(f32[96,4096]{0,1:T(8,128)} %get-tuple-element.21) | copy-start | bytes 4718596
Sparse Core Ops, SparseCore 0:
  9.5 40.1 all-gather.4
  51.3 17.4 all-gather.2
  74.9 74.4 reduce-scatter.4
  151.8 20.0 reduce-scatter.6
where the time goes:
time: 181 us; the launch traced here: 180 us
  waiting for transfers between devices  84 us (46%)
  local copies, waits for them, and re-layouts  27.2 us (15%)
  matrix products  22.4 us (12%)
  other arithmetic  19.4 us (11%)
  between operations  14.2 us (8%)
  starting transfers between devices  12.9 us (7%)
    reduce_scatter x1, waiting for transfers between devices, body(): lax.psum_scatter(full_grad, 'table', scatter_dimension=1, tiled=True)  26.4 us
    all_gather x1, waiting for transfers between devices, body(): full_uqkv = lax.all_gather(w_uqkv, 'replica', axis=0, tiled=True)  19.1 us
    unnamed x57, local copies, waits for them, and re-layouts  15.3 us
    all_to_all x1, waiting for transfers between devices, body(): lax.all_to_all(sending, 'table', split_axis=0, concat_axis=2, tiled=True)  13.1 us
    unnamed x5, waiting for transfers between devices  12.6 us
    all_gather x1, waiting for transfers between devices, body(): lax.all_gather(w_out, 'replica', axis=0, tiled=True)  8.68 us
    scatter-add x1, other arithmetic, body(): grad_cols = jnp.zeros_like(cache).at[:, slot_ids].add(returned)  7.41 us
    all_to_all x1, starting transfers between devices, body(): lax.all_to_all(picked, 'table', split_axis=1, concat_axis=0, tiled=True)  7.28 us
  transfers between devices with their start and end apart: 6, of which 6 were waited for; matrix products, arithmetic and copies ran while one was open for 32% of the time, Pallas kernels for 0%

commit v1 on v0

--- a/solution.py
+++ b/solution.py
@@ -13,6 +13,28 @@
 EPS_NORM = 1e-05
 EPS_ATTN = 1e-06
 STEP_SIZE = 0.5
+
+
+def laid_out(blocks, dim):
+    blocks = jnp.moveaxis(blocks, 0, dim)
+    dims = blocks.shape
+    return blocks.reshape(*dims[:dim], dims[dim] * dims[dim + 1], *dims[dim + 2 :])
+
+
+def ring_gather(array, axis, dim):
+    devices = lax.axis_size(axis)
+    pairs = [(i, (i + 1) % devices) for i in range(devices)]
+    back = [(b, a) for a, b in pairs]
+    lower, upper = ([], [])
+    for turn in range(devices - 1):
+        if turn % 2 == 0:
+            lower.append(lax.ppermute(lower[-1] if lower else array, axis, pairs))
+        else:
+            upper.append(lax.ppermute(upper[-1] if upper else array, axis, back))
+    tiles = jnp.stack([*lower[::-1], array, *upper])
+    shift = lax.axis_index(axis) - len(lower)
+    tiles = tiles[(jnp.arange(devices) - shift) % devices]
+    return laid_out(tiles, dim)
 
 
 def normalize(row_data):
@@ -77,7 +99,7 @@
     embedded = arrived.reshape(D, CAP).T
     row_float = embedded.astype(jnp.float32)
     normed = normalize(row_float).astype(jnp.bfloat16)
-    full_uqkv = lax.all_gather(w_uqkv, "replica", axis=0, tiled=True)
+    full_uqkv = ring_gather(w_uqkv, "replica", 0)
     hidden_pre = jnp.dot(normed, full_uqkv, preferred_element_type=jnp.float32)
     live_cot = cotangent[0] * inside.reshape(-1)[:, None].astype(jnp.bfloat16)
     d_gated = lax.dot_general(

time: 181 us -> 190 us (1.050)
  other arithmetic: 19.4 us -> 24.3 us
  local copies, waits for them, and re-layouts: 27.2 us -> 31.9 us
  waiting for transfers between devices: 84 us -> 81.7 us
    ppermute x0 -> x3, waiting for transfers between devices: none -> 28.8 us  [the longest x2 28.8 us: ring_gather(): lower.append(lax.ppermute(lower[-1] if lower else array, axis, pairs))]
    all_gather x1 -> x0, waiting for transfers between devices: 19.1 us -> none  [body(): full_uqkv = lax.all_gather(w_uqkv, 'replica', axis=0, tiled=True)]
    all_gather x1, waiting for transfers between devices: 8.68 us -> 0.01 us  [body(): lax.all_gather(w_out, 'replica', axis=0, tiled=True)]
    gather x0 -> x1, local copies, waits for them, and re-layouts: none -> 5.32 us  [ring_gather(): tiles = tiles[(jnp.arange(devices) - shift) % devices]]
    another operation x0 -> x1, other arithmetic: none -> 4.08 us  [ring_gather(): tiles = jnp.stack([*lower[::-1], array, *upper])]
    all_to_all x1, waiting for transfers between devices: 4.07 us -> 0.01 us  [body(): lax.all_to_all(picked, 'table', split_axis=1, concat_axis=0, tiled=True)]
    ppermute x0 -> x3, starting transfers between devices: none -> 2.49 us  [the longest x1 2.49 us: ring_gather(): upper.append(lax.ppermute(upper[-1] if upper else array, axis, back))]
    unnamed x5 -> x4, waiting for transfers between devices: 12.6 us -> 12.1 us
  transfers between devices with their start and end apart: 6 -> 8, of which waited for: 6 -> 5; matrix products, arithmetic and copies ran while one was open for 32% -> 36% of each run, Pallas kernels for 0% -> 0%
where the time goes in v1:
time: 190 us; the launch traced here: 189 us
  waiting for transfers between devices  81.7 us (43%)
  local copies, waits for them, and re-layouts  31.9 us (17%)
  other arithmetic  24.3 us (13%)
  matrix products  22.4 us (12%)
  starting transfers between devices  14.4 us (8%)
  between operations  14.2 us (7%)
    ppermute x2, waiting for transfers between devices, ring_gather(): lower.append(lax.ppermute(lower[-1] if lower else array, axis, pairs))  28.8 us
    reduce_scatter x1, waiting for transfers between devices, body(): lax.psum_scatter(full_grad, 'table', scatter_dimension=1, tiled=True)  27.5 us
    unnamed x55, local copies, waits for them, and re-layouts  15.3 us
    all_to_all x1, waiting for transfers between devices, body(): lax.all_to_all(sending, 'table', split_axis=0, concat_axis=2, tiled=True)  13.3 us
    unnamed x4, waiting for transfers between devices  12.1 us
    scatter-add x1, other arithmetic, body(): grad_cols = jnp.zeros_like(cache).at[:, slot_ids].add(returned)  7.42 us
    all_to_all x1, starting transfers between devices, body(): lax.all_to_all(sending, 'table', split_axis=0, concat_axis=2, tiled=True)  5.81 us
    all_to_all x1, starting transfers between devices, body(): lax.all_to_all(picked, 'table', split_axis=1, concat_axis=0, tiled=True)  5.81 us
  transfers between devices with their start and end apart: 8, of which 5 were waited for; matrix products, arithmetic and copies ran while one was open for 36% of the time, Pallas kernels for 0%

profile of v1, /device:TPU:0, one launch (start us, length us, event | category | flops | bytes accessed | tf_op | source)
XLA Modules:
  0.0 188.8 jit_solution(8978948444521933250)
XLA Ops:
  7.2 2.5 %collective-permute-start.2 = (bf16[192,3072]{1,0:T(8,128)(2,1)}, bf16[192,3072]{1,0:T(8,128)(2,1)}, u32[]{:S(2)}, u32[]{:S(2)}) collective-permute-start(bf16[192,3072]{1,0:T(8,128)(2,1)} %param.17), channel_id=1, source_target_pairs={{8,0},{16,8},{24,16},{0,24},{9,1},{17,9},{25,17},{1,25},{10,2},{18... | collective-permute-start | bytes 3538952 | tf_op jit(solution)/shard_map/ppermute | solution.py:33
  10.4 1.8 copy.119
  12.9 2.9 %gather_fusion.1 = bf16[1024,96]{1,0:T(8,128)(2,1)S(1)} fusion(f32[96,4096]{0,1:T(8,128)S(1)} %copy.119, s32[1024]{0:T(1024)S(1)} %broadcast_clamp_fusion), kind=kCustom, calls=%fused_computation.1 | custom fusion | bytes 397312 | tf_op jit(solution)/shard_map/jit(_take)/gather | solution.py:97
  16.7 5.8 %all-to-all-start = ((bf16[96,8,128]{2,0,1:T(8,128)(2,1)}), bf16[96,8,128]{2,0,1:T(8,128)(2,1)S(1)}, u32[]{:S(2)}, u32[]{:S(2)}) async-start(bf16[96,8,128]{2,0,1:T(8,128)(2,1)} %select_convert_fusion), calls=%async_computation | async-start | bytes 393216 | tf_op jit(solution)/shard_map/all_to_all | solution.py:98
  23.9 15.9 %collective-permute-done = bf16[192,3072]{1,0:T(8,128)(2,1)} collective-permute-done((bf16[192,3072]{1,0:T(8,128)(2,1)}, bf16[192,3072]{1,0:T(8,128)(2,1)}, u32[]{:S(2)}, u32[]{:S(2)}) %collective-permute-start) | collective-permute-done | bytes 1179680 | tf_op jit(solution)/shard_map/ppermute | solution.py:31
  43.4 12.9 %collective-permute-done.1 = bf16[192,3072]{1,0:T(8,128)(2,1)} collective-permute-done((bf16[192,3072]{1,0:T(8,128)(2,1)}, bf16[192,3072]{1,0:T(8,128)(2,1)}, u32[]{:S(2)}, u32[]{:S(2)}) %collective-permute-start.1) | collective-permute-done | bytes 1179680 | tf_op jit(solution)/shard_map/ppermute | solution.py:31
  56.3 4.1 %pad_maximum_fusion = bf16[4,192,3072]{2,1,0:T(8,128)(2,1)} fusion(bf16[1,192,3072]{2,1,0:T(8,128)(2,1)} %bitcast.18, bf16[1,192,3072]{2,1,0:T(8,128)(2,1)} %bitcast.130, bf16[1,192,3072]{2,1,0:T(8,128)(2,1)} %bitcast.16, bf16[1,192,3072]{2,1,0:T(8,128)(2,1)} %bitcast.15), kind=kLoop, calls=%fused_computation.5 | loop fusion | flops 7077888 | bytes 9437184 | tf_op jit(solution)/shard_map/stack | solution.py:34
  60.4 5.3 %gather_fusion.2 = bf16[4,192,3072]{2,1,0:T(8,128)(2,1)} fusion(bf16[4,192,3072]{2,1,0:T(8,128)(2,1)} %pad_maximum_fusion, s32[1024]{0:T(1024)S(1)} %pad_clamp_fusion), kind=kCustom, calls=%fused_computation.2 | custom fusion | bytes 9437200 | tf_op jit(solution)/shard_map/gather | solution.py:36
  65.7 4.4 %multiply_convert_fusion = (bf16[128,3072]{1,0:T(8,128)(2,1)S(1)}, f32[128,3072]{1,0:T(8,128)}) fusion(bf16[768,3072]{1,0:T(8,128)(2,1)} %bitcast.123, f32[768,128]{0,1:T(8,128)S(1)} %copy.103, f32[128]{0:T(128)S(1)} %get-tuple-element.31, f32[128]{0:T(128)S(1)} %broadcast_multiply_fusion.1), kind=kOutput, calls=%fused_computation.14 | convolution fusion | flops 606240768 | bytes 7472128 | tf_op jit(solution)/shard_map/dot_general | solution.py:103
  71.6 1.3 multiply_convert_fusion.1
  72.9 1.0 fusion.54
  75.4 1.9 %multiply_reduce_fusion = (f32[128]{0:T(128)S(1)}, f32[128,768]{1,0:T(8,128)S(1)}) fusion(f32[128,768]{1,0:T(8,128)S(1)} %copy.110, f32[128]{0:T(128)S(1)} %broadcast_multiply_fusion, bf16[128,3072]{1,0:T(8,128)(2,1)} %copy-done.2, bf16[768,768]{1,0:T(8,128)(2,1)} %all-gather.2.cloned.1.call-done, bf16[1,128,768]{2,1,0:T(8,128)(2,1)S(1)} %copy-done.3, ...), kind=kOutput, calls=%fused_computation.58 | convolution fusion | flops 151584640 | bytes 2360576 | tf_op jit(solution)/shard_map/dot_general | solution.py:105
  78.6 3.0 %fusion.28 = f32[768,768]{0,1:T(8,128)} fusion(f32[128,768]{1,0:T(8,128)S(1)} %copy.110, f32[128]{0:T(128)S(1)} %broadcast_multiply_fusion, f32[128]{0:T(128)S(1)} %get-tuple-element.33, bf16[1,128,768]{2,1,0:T(8,128)(2,1)S(1)} %copy-done.3, bf16[128,3072]{1,0:T(8,128)(2,1)} %copy-done.2, bf16[128]{0:T(256)(128)(2,1)S(1)} %fusion.50), kind=kOutput, calls=%fused_computation.61 | convolution fusion | flops 151584768 | bytes 3147008 | tf_op jit(solution)/shard_map/dot_general | solution.py:126
  81.6 1.8 fusion.52
  84.4 1.8 fusion.11
  86.2 1.1 fusion.56
  87.2 1.8 copy.114
  89.0 1.8 fusion.57
  90.8 1.8 copy.113
  92.6 1.2 fusion.55
  94.0 4.9 %fusion.25 = (f32[128]{0:T(128)S(1)}, f32[128,768]{1,0:T(8,128)S(1)}) fusion(f32[768,128]{0,1:T(8,128)S(1)} %copy.103, f32[128]{0:T(128)S(1)} %copy-done.22, f32[128]{0:T(128)S(1)} %copy-done.15, bf16[768,3072]{1,0:T(8,128)(2,1)} %bitcast.124, f32[128,3072]{1,0:T(8,128)} %get-tuple-element.35, bf16[128,768]{1,0:T(8,128)(2,1)S(1)} %copy-done.11, ...), kind=kOutput, calls=%fused_computation.55 | convolution fusion | flops 611450752 | bytes 7865856 | tf_op jit(solution)/shard_map/dot_general | solution.py:114
  100.3 5.8 %all-to-all-start.1 = ((f32[8,96,128]{2,1,0:T(8,128)}), f32[8,96,128]{2,1,0:T(8,128)S(1)}, u32[]{:S(2)}, u32[]{:S(2)}) async-start(f32[8,96,128]{2,1,0:T(8,128)} %bitcast.46), calls=%async_computation.1 | async-start | bytes 786432 | tf_op jit(solution)/shard_map/all_to_all | solution.py:120
  106.3 2.8 %copy.118 = f32[96,4096]{0,1:T(8,128)} copy(f32[96,4096]{1,0:T(8,128)} %param.11) | data formatting | bytes 3145728 | tf_op args[1]
  109.3 13.3 %all-to-all-done.1 = f32[8,96,128]{2,1,0:T(8,128)S(1)} async-done(((f32[8,96,128]{2,1,0:T(8,128)}), f32[8,96,128]{2,1,0:T(8,128)S(1)}, u32[]{:S(2)}, u32[]{:S(2)}) %all-to-all-start.1) | async-done | bytes 393248 | tf_op jit(solution)/shard_map/all_to_all | solution.py:120
  123.0 7.4 %scatter_custom_fusion = f32[96,4096]{0,1:T(8,128)} fusion(s32[1024]{0:T(1024)S(1)} %bitcast.145, f32[1024,96]{1,0:T(8,128)S(1)} %copy.117, f32[]{:T(128)} %constant.80.clone.1), kind=kCustom, calls=%fused_computation.24 | custom fusion | flops 98304 | bytes 1572868 | tf_op jit(solution)/shard_map/scatter-add | solution.py:123
  130.4 27.5 %reduce-scatter.5.cloned.1.call-done = f32[768,96]{0,1:T(8,128)} async-done(((f32[768,768]{0,1:T(8,128)}), f32[768,96]{0,1:T(8,128)}) %reduce-scatter.5.cloned.1.call-update) | async-done | bytes 294928 | tf_op jit(solution)/shard_map/reduce_scatter | solution.py:129
  158.0 1.9 %copy.124 = f32[768,96]{1,0:T(8,128)} copy(f32[768,96]{0,1:T(8,128)} %reduce-scatter.5.cloned.1.call-done) | data formatting | bytes 589824
  159.9 4.6 %multiply_subtract_fusion = (f32[96,4096]{0,1:T(8,128)}, f32[96,4096]{0,1:T(8,128)}) fusion(f32[96,4096]{0,1:T(8,128)S(1)} %copy.119, f32[96,4096]{0,1:T(8,128)} %scatter_custom_fusion, f32[96,4096]{0,1:T(8,128)} %copy.118), kind=kLoop, calls=%fused_computation.7 | loop fusion | flops 1966080 | bytes 7864320 | tf_op jit(solution)/shard_map/sub | solution.py:125
  164.5 2.9 %copy.121 = f32[96,4096]{1,0:T(8,128)} copy(f32[96,4096]{0,1:T(8,128)} %get-tuple-element.20) | data formatting | bytes 3145728
  167.5 1.7 copy.122
  169.2 11.4 %reduce-scatter.7.cloned.1.call-done = f32[192,96]{1,0:T(8,128)} async-done(((f32[768,96]{1,0:T(8,128)}), f32[192,96]{1,0:T(8,128)}) %reduce-scatter.7.cloned.1.call-update) | async-done | bytes 73744
  180.5 1.0 copy.125
  (109 shorter events, 15.3 us)
Async XLA Ops:
  7.2 5.1 %copy-start = (s32[1,8,128]{2,1,0:T(8,128)S(1)}, s32[1,8,128]{2,1,0:T(8,128)}, u32[]{:S(2)}) copy-start(s32[1,8,128]{2,1,0:T(8,128)} %param.12) | copy-start | bytes 12292
  7.2 36.2 %collective-permute-start.2 = (bf16[192,3072]{1,0:T(8,128)(2,1)}, bf16[192,3072]{1,0:T(8,128)(2,1)}, u32[]{:S(2)}, u32[]{:S(2)}) collective-permute-start(bf16[192,3072]{1,0:T(8,128)(2,1)} %param.17), channel_id=1, source_target_pairs={{8,0},{16,8},{24,16},{0,24},{9,1},{17,9},{25,17},{1,25},{10,2},{18... | collective-permute-start | bytes 3538952 | tf_op jit(solution)/shard_map/ppermute | solution.py:33
  9.7 30.1 %collective-permute-start = (bf16[192,3072]{1,0:T(8,128)(2,1)}, bf16[192,3072]{1,0:T(8,128)(2,1)}, u32[]{:S(2)}, u32[]{:S(2)}) collective-permute-start(bf16[192,3072]{1,0:T(8,128)(2,1)} %param.17), channel_id=1, source_target_pairs={{0,8},{8,16},{16,24},{24,0},{1,9},{9,17},{17,25},{25,1},{2,10},{10... | collective-permute-start | bytes 3538952 | tf_op jit(solution)/shard_map/ppermute | solution.py:31
  12.9 27.6 %copy-start.17 = (s32[1,8,2,2]{1,3,2,0:T(2,128)S(1)}, s32[1,8,2,2]{1,3,2,0:T(2,128)}, u32[]{:S(2)}) copy-start(s32[1,8,2,2]{1,3,2,0:T(2,128)} %param.15) | copy-start | bytes 388
  16.7 25.6 %all-to-all-start = ((bf16[96,8,128]{2,0,1:T(8,128)(2,1)}), bf16[96,8,128]{2,0,1:T(8,128)(2,1)S(1)}, u32[]{:S(2)}, u32[]{:S(2)}) async-start(bf16[96,8,128]{2,0,1:T(8,128)(2,1)} %select_convert_fusion), calls=%async_computation | async-start | bytes 393216 | tf_op jit(solution)/shard_map/all_to_all | solution.py:98
  22.5 52.9 %all-gather.2.cloned.1.call-start = ((), (), s32[]{:S(2)}) async-start(), calls=%async_computation.4 | async-start | bytes 1474560 | tf_op jit(solution)/shard_map/all_gather | solution.py:107
  23.2 134.7 %reduce-scatter.5.cloned.1.call-start = ((), (), s32[]{:S(2)}) async-start(), calls=%async_computation.5 | async-start | bytes 2654208 | tf_op jit(solution)/shard_map/reduce_scatter | solution.py:129
  39.8 16.5 %collective-permute-start.1 = (bf16[192,3072]{1,0:T(8,128)(2,1)}, bf16[192,3072]{1,0:T(8,128)(2,1)}, u32[]{:S(2)}, u32[]{:S(2)}) collective-permute-start(bf16[192,3072]{1,0:T(8,128)(2,1)} %collective-permute-done), channel_id=1, source_target_pairs={{0,8},{8,16},{16,24},{24,0},{1,9},{9,17},{17,25},{25,1},{2,10},{10... | collective-permute-start | bytes 3538952 | tf_op jit(solution)/shard_map/ppermute | solution.py:31
  42.7 23.1 %copy-start.14 = (f32[128]{0:T(128)}, f32[128]{0:T(128)S(1)}, u32[]{:S(2)}) copy-start(f32[128]{0:T(128)S(1)} %broadcast_multiply_fusion.1) | copy-start | bytes 1540
  42.9 17.6 %copy-start.20 = (f32[128]{0:T(128)}, f32[128]{0:T(128)S(1)}, u32[]{:S(2)}) copy-start(f32[128]{0:T(128)S(1)} %fusion.23) | copy-start | bytes 1540
  43.4 22.3 %copy-start.18 = (f32[128]{0:T(128)}, f32[128]{0:T(128)S(1)}, u32[]{:S(2)}) copy-start(f32[128]{0:T(128)S(1)} %get-tuple-element.31) | copy-start | bytes 1540
  70.1 0.9 copy-start.2
  71.2 1.7 copy-start.6
  71.4 1.5 copy-start.7
  71.5 1.3 copy-start.8
  72.9 1.0 copy-start.4
  72.9 2.5 %copy-start.3 = (bf16[1,128,768]{2,1,0:T(8,128)(2,1)S(1)}, bf16[1,128,768]{2,1,0:T(8,128)(2,1)}, u32[]{:S(2)}) copy-start(bf16[1,128,768]{2,1,0:T(8,128)(2,1)} %param.16) | copy-start | bytes 589828
  75.4 1.9 %copy-start.16 = (f32[128]{0:T(128)S(1)}, f32[128]{0:T(128)}, u32[]{:S(2)}) copy-start(f32[128]{0:T(128)} %fusion.22) | copy-start | bytes 1540
  78.0 0.6 copy-start.13
  83.7 0.7 copy-start.10
  84.4 1.8 copy-start.9
  86.2 6.5 %copy-start.5 = (bf16[12,128,128]{2,1,0:T(8,128)(2,1)S(1)}, bf16[12,128,128]{2,1,0:T(8,128)(2,1)}, u32[]{:S(2)}) copy-start(bf16[12,128,128]{2,1,0:T(8,128)(2,1)} %copy-done.4) | copy-start | bytes 1179652
  87.2 6.7 %copy-start.15 = (f32[128]{0:T(128)S(1)}, f32[128]{0:T(128)}, u32[]{:S(2)}) copy-start(f32[128]{0:T(128)} %copy-done.14) | copy-start | bytes 1540
  87.2 6.7 %copy-start.22 = (f32[128]{0:T(128)S(1)}, f32[128]{0:T(128)}, u32[]{:S(2)}) copy-start(f32[128]{0:T(128)} %get-tuple-element.30) | copy-start | bytes 1540
  90.8 3.1 %copy-start.11 = (bf16[128,768]{1,0:T(8,128)(2,1)S(1)}, bf16[128,768]{1,0:T(8,128)(2,1)}, u32[]{:S(2)}) copy-start(bf16[128,768]{1,0:T(8,128)(2,1)} %get-tuple-element.26) | copy-start | bytes 589828
  94.0 5.0 %copy-start.21 = (f32[128]{0:T(128)S(1)}, f32[128]{0:T(128)}, u32[]{:S(2)}) copy-start(f32[128]{0:T(128)} %copy-done.20) | copy-start | bytes 1540
  94.0 5.0 %copy-start.19 = (f32[128]{0:T(128)S(1)}, f32[128]{0:T(128)}, u32[]{:S(2)}) copy-start(f32[128]{0:T(128)} %copy-done.18) | copy-start | bytes 1540
  100.3 22.2 %all-to-all-start.1 = ((f32[8,96,128]{2,1,0:T(8,128)}), f32[8,96,128]{2,1,0:T(8,128)S(1)}, u32[]{:S(2)}, u32[]{:S(2)}) async-start(f32[8,96,128]{2,1,0:T(8,128)} %bitcast.46), calls=%async_computation.1 | async-start | bytes 786432 | tf_op jit(solution)/shard_map/all_to_all | solution.py:120
  106.1 3.1 %copy-start.12 = (f32[192,96]{1,0:T(8,128)S(1)}, f32[192,96]{1,0:T(8,128)}, u32[]{:S(2)}) copy-start(f32[192,96]{1,0:T(8,128)} %param.19) | copy-start | bytes 221188
  106.1 74.4 %reduce-scatter.7.cloned.1.call-start = ((), (), s32[]{:S(2)}) async-start(), calls=%async_computation.6 | async-start | bytes 491520
  164.5 2.9 %copy-start.1 = (f32[96,4096]{0,1:T(8,128)S(1)}, f32[96,4096]{0,1:T(8,128)}, u32[]{:S(2)}) copy-start(f32[96,4096]{0,1:T(8,128)} %get-tuple-element.21) | copy-start | bytes 4718596
Sparse Core Ops, SparseCore 0:
  24.9 20.4 all-gather.1
  81.7 76.2 reduce-scatter.4
  160.5 20.0 reduce-scatter.6
